TPU v7x, 128 devices: a whole 4x4x4 slice. The times are simulated.
128 devices in a mesh: tm: 16 (over x, y_lo, core), space: 8 (over z, y_hi).
Axes of the slice: x: 4, y: 4 (y_hi: 2, y_lo: 2; y = y_hi * 2 + y_lo), z: 4, core: 2. Of those that a mesh axis runs over, the one named last changes fastest.
Arguments:
- input_field: float32 [64, 32, 32, 1024], P('tm', None, 'space'), may hold values from -6 to 6
- cotangent: float32 [64, 32, 32, 1024], P('tm', None, 'space'), may hold values from -6 to 6
- spectral_weights: float32 [2, 2, 16, 32, 32], replicated, may hold values from -0.75 to 0.75
- conv_kernel: float32 [2, 3, 32, 32], replicated, may hold values from -0.625 to 0.625
- mode_list: int32 [16], replicated, may hold values from 0 to 31, as said below
Outputs:
- grad_input: float32 [64, 32, 32, 1024], P('tm', None, 'space')
- grad_spectral: float32 [2, 2, 16, 32, 32], P(None, None, 'tm')
- grad_kernel: float32 [2, 3, 32, 32], replicated
Inputs may be any that keep to these rules, and one draw needn't show every extreme that they name: `mode_list`: 16 distinct frequencies in ascending order, with 0 and 31 among them.
All inputs are finite; a program needn't handle non-finite values.
Results may differ from a plain program's by a relative error of at most 0.00014.
Values sent between devices are 32-bit elements; how exact they have to be, the bound alone decides.
No kernel may reach another device: no remote copies, remote signals or barrier semaphores. Data moves between devices by JAX's collectives and lax.ppermute only.
A program may use at most 128 MiB of HBM per device.

v0:
```python
import math
import jax
import jax.numpy as jnp
from jax import lax
from jax.sharding import PartitionSpec as P

HIGHEST = lax.Precision.HIGHEST


def extended(value, sides, width):
    for axis, dim in sides:
        size, length = (lax.axis_size(axis), value.shape[dim])
        up = [(i, (i + 1) % size) for i in range(size - 1)]
        down = [(j, i) for i, j in up]
        last = lax.slice_in_dim(value, length - width, length, axis=dim)
        initial = lax.slice_in_dim(value, 0, width, axis=dim)
        before = lax.ppermute(last, axis, up)
        after = lax.ppermute(initial, axis, down)
        value = jnp.concatenate([before, value, after], axis=dim)
    return value


def tables(mode_list, time_count, total_time):
    time_steps = jnp.arange(time_count, dtype=jnp.int32)
    phase_index = mode_list[:, None] * time_steps[None, :] % total_time
    angles = phase_index.astype(jnp.float32) * (2.0 * math.pi / total_time)
    return (jnp.cos(angles), jnp.sin(angles))


def forward_dft(cosine_table, sine_table, flattened):
    time_count = flattened.shape[0]
    rows = flattened.reshape(time_count, -1)
    cosine_part = jnp.dot(cosine_table, rows, precision=HIGHEST)
    sine_part = -jnp.dot(sine_table, rows, precision=HIGHEST)
    stacked = jnp.stack([cosine_part, sine_part], axis=1)
    return stacked.reshape(cosine_table.shape[0], 2, flattened.shape[1], flattened.shape[2])


def inverse_dft(cosine_table, sine_table, coefficients, factor):
    mode_count = coefficients.shape[0]
    cosine_term = jnp.dot(
        cosine_table.T, coefficients[:, 0].reshape(mode_count, -1), precision=HIGHEST
    )
    sine_term = jnp.dot(sine_table.T, coefficients[:, 1].reshape(mode_count, -1), precision=HIGHEST)
    result = factor * (cosine_term - sine_term)
    return result.reshape(cosine_table.shape[1], coefficients.shape[2], coefficients.shape[3])


def mode_product(values, weight):
    return jnp.einsum("mcn,mcd->mdn", values, weight, precision=HIGHEST)


def mode_adjoint(values, weight):
    return jnp.einsum("mdn,mcd->mcn", values, weight, precision=HIGHEST)


def mode_outer(left_values, right_values):
    return jnp.einsum("mcn,mdn->mcd", left_values, right_values, precision=HIGHEST)


def channel_mix(coefficients, weight):
    real_part = mode_product(coefficients[:, 0], weight[0]) - mode_product(
        coefficients[:, 1], weight[1]
    )
    imag_part = mode_product(coefficients[:, 1], weight[0]) + mode_product(
        coefficients[:, 0], weight[1]
    )
    return jnp.stack([real_part, imag_part], axis=1)


def channel_mix_adjoint(sens_modes, weight):
    real_part = mode_adjoint(sens_modes[:, 0], weight[0]) + mode_adjoint(
        sens_modes[:, 1], weight[1]
    )
    imag_part = mode_adjoint(sens_modes[:, 1], weight[0]) - mode_adjoint(
        sens_modes[:, 0], weight[1]
    )
    return jnp.stack([real_part, imag_part], axis=1)


def weight_grad(coefficients, sens_modes):
    real_part = mode_outer(coefficients[:, 0], sens_modes[:, 0]) + mode_outer(
        coefficients[:, 1], sens_modes[:, 1]
    )
    imag_part = mode_outer(coefficients[:, 0], sens_modes[:, 1]) - mode_outer(
        coefficients[:, 1], sens_modes[:, 0]
    )
    return jnp.stack([real_part, imag_part], axis=0)


def convolve(padded, kernel, cells_x):
    result = jnp.einsum("tcxs,cd->tdxs", padded[:, :, 0:cells_x], kernel[0], precision=HIGHEST)
    for offset in range(1, 3):
        result = result + jnp.einsum(
            "tcxs,cd->tdxs",
            padded[:, :, offset : offset + cells_x],
            kernel[offset],
            precision=HIGHEST,
        )
    return result


def convolve_adjoint(sens_padded, kernel, cells_x):
    result = jnp.einsum(
        "tdxs,cd->tcxs", sens_padded[:, :, 2 : 2 + cells_x], kernel[0], precision=HIGHEST
    )
    for offset in range(1, 3):
        result = result + jnp.einsum(
            "tdxs,cd->tcxs",
            sens_padded[:, :, 2 - offset : 2 - offset + cells_x],
            kernel[offset],
            precision=HIGHEST,
        )
    return result


def gelu_exact(values):
    return jax.nn.gelu(values, approximate=False)


def on_device(input_field, cotangent, spectral_weights, conv_kernel, mode_list):
    groups = lax.axis_size("tm")
    total_time = input_field.shape[0] * groups
    layers = conv_kernel.shape[0]
    factor = 2.0 / total_time
    cosine_all, sine_all = tables(mode_list, total_time, total_time)
    state_field, gradient = (input_field, cotangent)
    time_local, channels, cells_x, cells_s = state_field.shape
    cell_count = cells_x * cells_s
    saved = []
    for layer_number in range(layers):
        padded = extended(state_field, (("space", 2),), 1)
        convolved = convolve(padded, conv_kernel[layer_number], cells_x)
        flattened = state_field.reshape(time_local, channels, cell_count)
        series_field = lax.all_to_all(flattened, "tm", split_axis=2, concat_axis=0, tiled=True)
        coefficients = forward_dft(cosine_all, sine_all, series_field)
        mixed = channel_mix(coefficients, spectral_weights[layer_number])
        returned = inverse_dft(cosine_all, sine_all, mixed, factor)
        spectral_part = lax.all_to_all(returned, "tm", split_axis=0, concat_axis=2, tiled=True)
        preact = spectral_part.reshape(state_field.shape) + convolved
        saved.append((padded, coefficients, preact))
        state_field = gelu_exact(preact)
    kernel_pieces = []
    mode_pieces = []
    for layer_number in reversed(range(layers)):
        padded, coefficients, preact = saved[layer_number]
        pullback = jax.vjp(gelu_exact, preact)[1]
        sensitivity = pullback(gradient)[0]
        kernel_piece = jnp.stack(
            [
                jnp.einsum(
                    "tcxs,tdxs->cd",
                    padded[:, :, offset : offset + cells_x],
                    sensitivity,
                    precision=HIGHEST,
                )
                for offset in range(3)
            ]
        )
        sens_padded = extended(sensitivity, (("space", 2),), 1)
        back_conv = convolve_adjoint(sens_padded, conv_kernel[layer_number], cells_x)
        flat_sens = sensitivity.reshape(time_local, channels, cell_count)
        series_sens = lax.all_to_all(flat_sens, "tm", split_axis=2, concat_axis=0, tiled=True)
        sens_modes = factor * forward_dft(cosine_all, sine_all, series_sens)
        mode_piece = weight_grad(coefficients, sens_modes)
        adjoint = channel_mix_adjoint(sens_modes, spectral_weights[layer_number])
        returned = inverse_dft(cosine_all, sine_all, adjoint, 1.0)
        back_spec = lax.all_to_all(returned, "tm", split_axis=0, concat_axis=2, tiled=True)
        gradient = back_spec.reshape(sensitivity.shape) + back_conv
        kernel_pieces.append(kernel_piece)
        mode_pieces.append(mode_piece)
    kernel_total = lax.psum(jnp.stack(kernel_pieces[::-1]), ("tm", "space"))
    mode_stack = lax.psum_scatter(
        jnp.stack(mode_pieces[::-1]), "tm", scatter_dimension=2, tiled=True
    )
    mode_total = lax.psum(mode_stack, "space")
    return (gradient, mode_total, kernel_total)


def solution(mesh):
    placed = (P("tm", None, "space", None), P("tm", None, "space", None), P(), P(), P())
    return jax.shard_map(
        on_device,
        mesh=mesh,
        in_specs=placed,
        out_specs=(P("tm", None, "space", None), P(None, None, "tm", None, None), P()),
        check_vma=False,
    )
```

profile of v0, /device:TPU:0, one launch (start us, length us, event | category | flops | bytes accessed | tf_op | source)
XLA Modules:
  0.0 852.2 jit_solution(5890445966441035744)
XLA Ops:
  7.2 7.8 copy.219
  14.9 8.5 reshape.161
  23.4 33.1 %all_to_all.120 = f32[16,1,32768]{2,1,0:T(1,128)} all-to-all(f32[16,1,32768]{2,1,0:T(1,128)S(1)} %reshape.161), channel_id=1, replica_groups=mesh['tm'=16,'space'=8] {'tm'}, dimensions={0} | all-to-all | bytes 4194304 | tf_op jit(solution)/shard_map/all_to_all | solution.py:135
  57.0 7.3 reduce
  70.7 6.9 copy.330
  108.9 23.0 %collective-permute-done = f32[4,32,1,1024]{3,1,2,0:T(8,128)S(1)} collective-permute-done((f32[4,32,1,1024]{3,1,2,0:T(8,128)S(1)}, f32[4,32,1,1024]{3,1,2,0:T(8,128)S(1)}, u32[]{:S(2)}, u32[]{:S(2)}) %collective-permute-start) | collective-permute-done | bytes 524320 | tf_op jit(solution)/shard_map/ppermute | solution.py:17
  134.9 11.6 %collective-permute-done.1 = f32[4,32,1,1024]{3,1,2,0:T(8,128)S(1)} collective-permute-done((f32[4,32,1,1024]{3,1,2,0:T(8,128)S(1)}, f32[4,32,1,1024]{3,1,2,0:T(8,128)S(1)}, u32[]{:S(2)}, u32[]{:S(2)}) %collective-permute-start.1) | collective-permute-done | bytes 524320 | tf_op jit(solution)/shard_map/ppermute | solution.py:18
  155.9 10.0 %multiply_multiply_fusion.10 = (f32[4,32,4,1024]{3,1,2,0:T(8,128)S(1)}, f32[4,32,4,1024]{3,1,2,0:T(8,128)}) fusion(f32[4,32,5,1024]{3,1,2,0:T(8,128)} %constant_dynamic-update-slice_fusion.2, f32[2,3,32,32]{3,2,1,0:T(8,128)S(1)} %copy-done.28, f32[32,4,4,1024]{3,0,2,1:T(8,128)} %fusion.154, f32[4,4,1024,32]{2,3,1,0:T(8,128)} %fusion.157, ...), kind=kOutput, calls=%fused_computation.86 | convolution fusion | flops 236453888 | bytes 13123584 | tf_op jit(solution)/shard_map/tcxs,cd->tdxs/dot_general | solution.py:94
  171.8 9.5 %reshape.163 = f32[16,1,32768]{2,1,0:T(1,128)} reshape(f32[4096,4,32]{2,1,0:T(4,128)} %bitcast.414) | data formatting | bytes 4194304
  181.3 32.7 %all_to_all.121 = f32[16,1,32768]{2,1,0:T(1,128)} all-to-all(f32[16,1,32768]{2,1,0:T(1,128)} %reshape.163), channel_id=1, replica_groups=mesh['tm'=16,'space'=8] {'tm'}, dimensions={0} | all-to-all | bytes 4194304 | tf_op jit(solution)/shard_map/all_to_all | solution.py:135
  214.0 8.6 %reduce.1 = f32[16,32768]{1,0:T(8,128)} reduce(f32[16,1,32768]{2,1,0:T(1,128)} %all_to_all.121, f32[]{:T(128)} %broadcast.353), dimensions={1}, to_apply=%all_to_all.94.reduce_sub_computation | reduce | bytes 4194308 | tf_op jit(solution)/shard_map/all_to_all | solution.py:135
  222.6 7.7 reshape.164
  230.3 8.4 copy.239
  270.5 23.8 %collective-permute-done.2 = f32[4,32,1,1024]{3,1,2,0:T(8,128)S(1)} collective-permute-done((f32[4,32,1,1024]{3,1,2,0:T(8,128)S(1)}, f32[4,32,1,1024]{3,1,2,0:T(8,128)S(1)}, u32[]{:S(2)}, u32[]{:S(2)}) %collective-permute-start.2) | collective-permute-done | bytes 524320 | tf_op jit(solution)/shard_map/ppermute | solution.py:17
  309.3 10.8 %fusion.26 = f32[4,32,4,1024]{3,1,2,0:T(8,128)} fusion(f32[4,32,4,1024]{3,2,1,0:T(4,128)} %param.6, f32[4,4,1024,32]{2,3,1,0:T(8,128)} %fusion.20, f32[4,4,1024,32]{2,3,1,0:T(8,128)} %fusion.142, f32[4,32,4,1024]{3,2,1,0:T(4,128)} %reshape.128, f32[4,32,1,1024]{3,1,2,0:T(8,128)} %collective-permute-done.3, f32[4,32,4,1024]{3,1,2,0:T(8,128)S(1)} %get-tuple-element.29, ...), kind=kOutput, calls=%fused_computation.38 | convolution fusion | flops 240779264 | bytes 13123584 | tf_op jit(solution)/shard_map/tcxs,cd->tdxs/dot_general | solution.py:94
  320.1 7.8 copy.332
  328.0 9.5 %reshape.165 = f32[16,1,32768]{2,1,0:T(1,128)} reshape(f32[4096,4,32]{2,1,0:T(4,128)} %bitcast.415) | data formatting | bytes 4194304
  337.5 32.9 %all_to_all.122 = f32[16,1,32768]{2,1,0:T(1,128)} all-to-all(f32[16,1,32768]{2,1,0:T(1,128)} %reshape.165), channel_id=1, replica_groups=mesh['tm'=16,'space'=8] {'tm'}, dimensions={0} | all-to-all | bytes 4194304 | tf_op jit(solution)/shard_map/all_to_all | solution.py:163
  370.4 8.6 %reduce.2 = f32[16,32768]{1,0:T(8,128)} reduce(f32[16,1,32768]{2,1,0:T(1,128)} %all_to_all.122, f32[]{:T(128)} %broadcast.353), dimensions={1}, to_apply=%all_to_all.100.reduce_sub_computation | reduce | bytes 4194308 | tf_op jit(solution)/shard_map/all_to_all | solution.py:163
  379.0 7.7 reshape.166
  386.7 8.4 copy.254
  421.4 6.8 collective-permute-start.5
  438.2 17.2 %collective-permute-done.4 = f32[4,32,1,1024]{3,1,2,0:T(8,128)S(1)} collective-permute-done((f32[4,32,1,1024]{3,1,2,0:T(8,128)S(1)}, f32[4,32,1,1024]{3,1,2,0:T(8,128)S(1)}, u32[]{:S(2)}, u32[]{:S(2)}) %collective-permute-start.4) | collective-permute-done | bytes 524320 | tf_op jit(solution)/shard_map/ppermute | solution.py:18
  464.0 9.6 %multiply_add_fusion = f32[4,32,4,1024]{3,1,2,0:T(8,128)S(1)} fusion(f32[4,32,4,1024]{3,2,1,0:T(4,128)} %reshape.133, f32[4,4,1024,32]{2,3,1,0:T(8,128)} %fusion.2, f32[4,4,1024,32]{2,3,1,0:T(8,128)} %fusion.140, f32[4,32,4,1024]{3,1,2,0:T(8,128)} %get-tuple-element.30, f32[4,32,4,1024]{3,1,2,0:T(8,128)} %fusion.26, ...), kind=kOutput, calls=%fused_computation.57 | convolution fusion | flops 240779264 | bytes 13123584 | tf_op jit(solution)/shard_map/tdxs,cd->tcxs/dot_general | solution.py:108
  479.6 9.5 %reshape.167 = f32[16,1,32768]{2,1,0:T(1,128)} reshape(f32[4096,4,32]{2,1,0:T(4,128)} %bitcast.416) | data formatting | bytes 4194304
  504.0 7.3 collective-permute-start.7
  522.0 8.6 %reduce.3 = f32[16,32768]{1,0:T(8,128)} reduce(f32[16,1,32768]{2,1,0:T(1,128)} %all-to-all-done.6, f32[]{:T(128)} %broadcast.353), dimensions={1}, to_apply=%all_to_all.106.reduce_sub_computation | reduce | bytes 4194308 | tf_op jit(solution)/shard_map/all_to_all | solution.py:163
  530.6 7.7 reshape.168
  538.3 8.1 copy.272
  569.6 88.0 %psum.15 = f32[2,3,32,32]{3,2,1,0:T(8,128)} all-reduce(f32[2,3,32,32]{3,2,1,0:T(8,128)S(1)} %pad_maximum_fusion.11), channel_id=1, replica_groups=mesh['tm'=16,'space'=8] {'tm','space'}, use_global_device_ids=true, to_apply=%region_2.3 | all-reduce | flops 6144 | bytes 49152 | tf_op jit(solution)/shard_map/psum | solution.py:172
  671.1 112.7 %all-reduce.3.cloned.1.call-done = f32[2,2,16,32,32]{4,3,2,1,0:T(8,128)} async-done(((f32[2,2,16,32,32]{4,3,2,1,0:T(8,128)}), f32[2,2,16,32,32]{4,3,2,1,0:T(8,128)}) %all-reduce.3.cloned.1.call-update) | async-done | bytes 262160
  785.1 43.4 %psum.14 = f32[2,2,1,32,32]{4,3,2,1,0:T(8,128)} all-reduce(f32[2,2,1,32,32]{4,3,2,1,0:T(8,128)S(1)} %constant_dynamic-slice_fusion), channel_id=1, replica_groups=mesh['tm'=16,'space'=8] {'space'}, use_global_device_ids=true, to_apply=%region_1.2 | all-reduce | flops 4096 | bytes 32768 | tf_op jit(solution)/shard_map/psum | solution.py:176
  (198 shorter events, 233.0 us)
Async XLA Ops:
  81.2 5.9 copy-start.11
  92.8 4.6 copy-start.1
  92.8 58.0 %all-to-all-start.1 = ((f32[64,32,256]{2,1,0:T(8,128)}), f32[64,32,256]{2,1,0:T(8,128)}, u32[]{:S(2)}, u32[]{:S(2)}) async-start(f32[64,32,256]{2,1,0:T(8,128)} %bitcast.439), calls=%async_computation.1 | async-start | bytes 4194304 | tf_op jit(solution)/shard_map/all_to_all | solution.py:139
  97.4 7.2 copy-start.28
  98.3 33.6 %collective-permute-start = (f32[4,32,1,1024]{3,1,2,0:T(8,128)S(1)}, f32[4,32,1,1024]{3,1,2,0:T(8,128)S(1)}, u32[]{:S(2)}, u32[]{:S(2)}) collective-permute-start(f32[4,32,1,1024]{3,1,2,0:T(8,128)S(1)} %copy.463), channel_id=1, source_target_pairs={{0,1},{1,2},{2,3},{3,4},{4,5},{5,6},{6,7},{8,9},{9,10},{10,11},{11... | collective-permute-start | bytes 1572872 | tf_op jit(solution)/shard_map/ppermute | solution.py:17
  103.2 43.2 %collective-permute-start.1 = (f32[4,32,1,1024]{3,1,2,0:T(8,128)S(1)}, f32[4,32,1,1024]{3,1,2,0:T(8,128)S(1)}, u32[]{:S(2)}, u32[]{:S(2)}) collective-permute-start(f32[4,32,1,1024]{3,1,2,0:T(8,128)S(1)} %copy.464), channel_id=1, source_target_pairs={{1,0},{2,1},{3,2},{4,3},{5,4},{6,5},{7,6},{9,8},{10,9},{11,10},{12... | collective-permute-start | bytes 1572872 | tf_op jit(solution)/shard_map/ppermute | solution.py:18
  134.9 12.5 %copy-start.23 = (f32[4,32,5,1024]{3,1,2,0:T(8,128)}, f32[4,32,5,1024]{3,1,2,0:T(8,128)S(1)}, u32[]{:S(2)}) copy-start(f32[4,32,5,1024]{3,1,2,0:T(8,128)S(1)} %get-tuple-element.24) | copy-start | bytes 7864324
  238.7 4.0 copy-start.3
  242.7 7.1 copy-start.13
  255.3 43.1 %all-to-all-start.3 = ((f32[64,32,256]{2,1,0:T(8,128)}), f32[64,32,256]{2,1,0:T(8,128)}, u32[]{:S(2)}, u32[]{:S(2)}) async-start(f32[64,32,256]{2,1,0:T(8,128)} %bitcast.440), calls=%async_computation.3 | async-start | bytes 4194304 | tf_op jit(solution)/shard_map/all_to_all | solution.py:139
  260.7 33.6 %collective-permute-start.2 = (f32[4,32,1,1024]{3,1,2,0:T(8,128)S(1)}, f32[4,32,1,1024]{3,1,2,0:T(8,128)S(1)}, u32[]{:S(2)}, u32[]{:S(2)}) collective-permute-start(f32[4,32,1,1024]{3,1,2,0:T(8,128)S(1)} %get-tuple-element.20), channel_id=1, source_target_pairs={{0,1},{1,2},{2,3},{3,4},{4,5},{5,6},{6,7},{8,9},{9,10},{10,11},{11... | collective-permute-start | bytes 1572872 | tf_op jit(solution)/shard_map/ppermute | solution.py:17
  265.8 43.5 %collective-permute-start.3 = (f32[4,32,1,1024]{3,1,2,0:T(8,128)}, f32[4,32,1,1024]{3,1,2,0:T(8,128)}, u32[]{:S(2)}, u32[]{:S(2)}) collective-permute-start(f32[4,32,1,1024]{3,1,2,0:T(8,128)} %get-tuple-element.19), channel_id=1, source_target_pairs={{1,0},{2,1},{3,2},{4,3},{5,4},{6,5},{7,6},{9,8},{10,9},{11,10},{12... | collective-permute-start | bytes 1572872 | tf_op jit(solution)/shard_map/ppermute | solution.py:18
  402.2 5.1 copy-start.17
  412.7 4.6 copy-start.32
  412.7 46.2 %all-to-all-start.5 = ((f32[64,32,256]{2,1,0:T(8,128)}), f32[64,32,256]{2,1,0:T(8,128)}, u32[]{:S(2)}, u32[]{:S(2)}) async-start(f32[64,32,256]{2,1,0:T(8,128)} %bitcast.438), calls=%async_computation.5 | async-start | bytes 4194304 | tf_op jit(solution)/shard_map/all_to_all | solution.py:168
  417.3 10.9 %copy-start = (f32[4,32,4,1024]{3,1,2,0:T(8,128)S(1)}, f32[4,32,4,1024]{3,1,2,0:T(8,128)}, u32[]{:S(2)}) copy-start(f32[4,32,4,1024]{3,1,2,0:T(8,128)} %fusion.26) | copy-start | bytes 6291460
  420.1 35.4 %collective-permute-start.4 = (f32[4,32,1,1024]{3,1,2,0:T(8,128)S(1)}, f32[4,32,1,1024]{3,1,2,0:T(8,128)S(1)}, u32[]{:S(2)}, u32[]{:S(2)}) collective-permute-start(f32[4,32,1,1024]{3,1,2,0:T(8,128)S(1)} %get-tuple-element.18), channel_id=1, source_target_pairs={{1,0},{2,1},{3,2},{4,3},{5,4},{6,5},{7,6},{9,8},{10,9},{11,10},{12... | collective-permute-start | bytes 1572872 | tf_op jit(solution)/shard_map/ppermute | solution.py:18
  421.4 42.6 %collective-permute-start.5 = (f32[4,32,1,1024]{3,1,2,0:T(8,128)}, f32[4,32,1,1024]{3,1,2,0:T(8,128)}, u32[]{:S(2)}, u32[]{:S(2)}) collective-permute-start(f32[4,32,1,1024]{3,1,2,0:T(8,128)} %get-tuple-element.17), channel_id=1, source_target_pairs={{0,1},{1,2},{2,3},{3,4},{4,5},{5,6},{6,7},{8,9},{9,10},{10,11},{11... | collective-permute-start | bytes 1572872 | tf_op jit(solution)/shard_map/ppermute | solution.py:17
  489.0 33.0 %all-to-all-start.6 = ((f32[16,1,32768]{2,1,0:T(1,128)}), f32[16,1,32768]{2,1,0:T(1,128)}, u32[]{:S(2)}, u32[]{:S(2)}) async-start(f32[16,1,32768]{2,1,0:T(1,128)} %reshape.167), calls=%async_computation.6 | async-start | bytes 4194304 | tf_op jit(solution)/shard_map/all_to_all | solution.py:163
  494.2 4.6 copy-start.14
  494.2 4.6 copy-start.18
  494.2 5.8 copy-start.10
  494.2 5.8 copy-start.16
  500.1 11.2 %copy-start.2 = (f32[4,32,4,1024]{3,2,1,0:T(4,128)S(1)}, f32[4,32,4,1024]{3,2,1,0:T(4,128)}, u32[]{:S(2)}) copy-start(f32[4,32,4,1024]{3,2,1,0:T(4,128)} %param.5) | copy-start | bytes 6291460
  502.7 163.9 %collective-permute-start.6 = (f32[4,32,1,1024]{3,1,2,0:T(8,128)}, f32[4,32,1,1024]{3,1,2,0:T(8,128)}, u32[]{:S(2)}, u32[]{:S(2)}) collective-permute-start(f32[4,32,1,1024]{3,1,2,0:T(8,128)} %get-tuple-element.16), channel_id=1, source_target_pairs={{1,0},{2,1},{3,2},{4,3},{5,4},{6,5},{7,6},{9,8},{10,9},{11,10},{12... | collective-permute-start | bytes 1572872 | tf_op jit(solution)/shard_map/ppermute | solution.py:18
  504.0 331.9 %collective-permute-start.7 = (f32[4,32,1,1024]{3,1,2,0:T(8,128)}, f32[4,32,1,1024]{3,1,2,0:T(8,128)}, u32[]{:S(2)}, u32[]{:S(2)}) collective-permute-start(f32[4,32,1,1024]{3,1,2,0:T(8,128)} %get-tuple-element.15), channel_id=1, source_target_pairs={{0,1},{1,2},{2,3},{3,4},{4,5},{5,6},{6,7},{8,9},{9,10},{10,11},{11... | collective-permute-start | bytes 1572872 | tf_op jit(solution)/shard_map/ppermute | solution.py:17
  514.1 3.6 copy-start.24
  553.6 5.1 copy-start.21
  564.1 5.4 copy-start.29
  564.1 264.4 %all-to-all-start.7 = ((f32[64,32,256]{2,1,0:T(8,128)}), f32[64,32,256]{2,1,0:T(8,128)}, u32[]{:S(2)}, u32[]{:S(2)}) async-start(f32[64,32,256]{2,1,0:T(8,128)} %bitcast.437), calls=%async_computation.7 | async-start | bytes 4194304 | tf_op jit(solution)/shard_map/all_to_all | solution.py:168
  569.5 214.2 %all-reduce.3.cloned.1.call-start = ((), (), s32[]{:S(2)}) async-start(), calls=%async_computation.8 | async-start | bytes 2097152
  657.6 4.7 copy-start.22
  (15 other events, 35.9 us)
Sparse Core Ops, SparseCore 0:
  666.7 117.0 all-reduce.2
where the time goes:
time: 862 us; the launch traced here: 852 us
  blocking collectives  230 us (27%)
  waiting for transfers between devices  194 us (23%)
  local copies, waits for them, and re-layouts  186 us (22%)
  matrix products  138 us (16%)
  starting transfers between devices  53.3 us (6%)
  other arithmetic  35.2 us (4%)
  between operations  15.6 us (2%)
    unnamed x2, waiting for transfers between devices  113 us
    unnamed x102, local copies, waits for them, and re-layouts  103 us
    psum x1, blocking collectives, on_device(): kernel_total = lax.psum(jnp.stack(kernel_pieces[::-1]), ('tm', 'space'))  88 us
    all_to_all x2, blocking collectives, on_device(): lax.all_to_all(flattened, 'tm', split_axis=2, concat_axis=0, tiled=True)  65.8 us
    ppermute x4, waiting for transfers between devices, extended(): before = lax.ppermute(last, axis, up)  46.8 us
    psum x1, blocking collectives, on_device(): mode_total = lax.psum(mode_stack, 'space')  43.4 us
    all_to_all x1, blocking collectives, on_device(): lax.all_to_all(flat_sens, 'tm', split_axis=2, concat_axis=0, tiled=True)  32.9 us
    ppermute x4, waiting for transfers between devices, extended(): after = lax.ppermute(initial, axis, down)  32.3 us
  transfers between devices with their start and end apart: 14, of which 7 were waited for; matrix products, arithmetic and copies ran while one was open for 15% of the time, Pallas kernels for 0%

commit v1 on v0

--- a/solution.py
+++ b/solution.py
@@ -160,7 +160,12 @@
         sens_padded = extended(sensitivity, (("space", 2),), 1)
         back_conv = convolve_adjoint(sens_padded, conv_kernel[layer_number], cells_x)
         flat_sens = sensitivity.reshape(time_local, channels, cell_count)
-        series_sens = lax.all_to_all(flat_sens, "tm", split_axis=2, concat_axis=0, tiled=True)
+        series_sens = jnp.concatenate(
+            lax.all_to_all(
+                jnp.stack(jnp.split(flat_sens, lax.axis_size("tm"), axis=2)), "tm", 0, 0
+            ),
+            axis=0,
+        )
         sens_modes = factor * forward_dft(cosine_all, sine_all, series_sens)
         mode_piece = weight_grad(coefficients, sens_modes)
         adjoint = channel_mix_adjoint(sens_modes, spectral_weights[layer_number])

time: 862 us -> 789 us (0.915)
  local copies, waits for them, and re-layouts: 186 us -> 134 us
  other arithmetic: 35.2 us -> 18 us
    unnamed x102 -> x124, local copies, waits for them, and re-layouts: 103 us -> 79.7 us
    all_to_all x2 -> x0, other arithmetic: 17.2 us -> none  [on_device(): lax.all_to_all(flat_sens, 'tm', split_axis=2, concat_axis=0, tiled=True)]
    all_to_all x2 -> x0, local copies, waits for them, and re-layouts: 16.5 us -> none  [on_device(): lax.all_to_all(flat_sens, 'tm', split_axis=2, concat_axis=0, tiled=True)]
    reshape x2, local copies, waits for them, and re-layouts: 13.8 us -> 0.37 us  [on_device(): flat_sens = sensitivity.reshape(time_local, channels, cell_count)]
  transfers between devices with their start and end apart: 14 -> 14, of which waited for: 7 -> 7; matrix products, arithmetic and copies ran while one was open for 15% -> 14% of each run, Pallas kernels for 0% -> 0%
where the time goes in v1:
time: 789 us; the launch traced here: 781 us
  blocking collectives  230 us (29%)
  waiting for transfers between devices  193 us (24%)
  matrix products  138 us (17%)
  local copies, waits for them, and re-layouts  134 us (17%)
  starting transfers between devices  53.3 us (7%)
  other arithmetic  18 us (2%)
  between operations  15.5 us (2%)
    unnamed x2, waiting for transfers between devices  113 us
    psum x1, blocking collectives, on_device(): kernel_total = lax.psum(jnp.stack(kernel_pieces[::-1]), ('tm', 'space'))  88 us
    unnamed x124, local copies, waits for them, and re-layouts  79.7 us
    all_to_all x2, blocking collectives, on_device(): lax.all_to_all(flattened, 'tm', split_axis=2, concat_axis=0, tiled=True)  65.8 us
    ppermute x4, waiting for transfers between devices, extended(): before = lax.ppermute(last, axis, up)  46.8 us
    psum x1, blocking collectives, on_device(): mode_total = lax.psum(mode_stack, 'space')  43.4 us
    all_to_all x1, blocking collectives, on_device(): lax.all_to_all(jnp.stack(jnp.split(flat_sens, lax.axis_size('tm'), axis=2...  32.4 us
    ppermute x4, waiting for transfers between devices, extended(): after = lax.ppermute(initial, axis, down)  31.3 us
  transfers between devices with their start and end apart: 14, of which 7 were waited for; matrix products, arithmetic and copies ran while one was open for 14% of the time, Pallas kernels for 0%

profile of v1, /device:TPU:0, one launch (start us, length us, event | category | flops | bytes accessed | tf_op | source)
XLA Modules:
  0.0 780.6 jit_solution(12259969831530154544)
XLA Ops:
  7.2 7.8 %copy.215 = f32[4,32,4,1024]{1,0,3,2:T(4,128)} copy(f32[4,32,4,1024]{3,2,1,0:T(4,128)} %param.5) | data formatting | bytes 4194304 | tf_op args[0]
  15.0 8.5 %reshape.151 = f32[16,1,32768]{2,1,0:T(1,128)S(1)} reshape(f32[4096,4,32]{2,1,0:T(4,128)} %bitcast.535) | data formatting | bytes 4194304
  23.5 33.1 %all_to_all.100 = f32[16,1,32768]{2,1,0:T(1,128)} all-to-all(f32[16,1,32768]{2,1,0:T(1,128)S(1)} %reshape.151), channel_id=1, replica_groups=mesh['tm'=16,'space'=8] {'tm'}, dimensions={0} | all-to-all | bytes 4194304 | tf_op jit(solution)/shard_map/all_to_all | solution.py:135
  57.1 7.3 reduce
  64.4 6.4 reshape.152
  70.8 6.8 copy.322
  92.6 4.6 all-to-all-start.1
  98.1 4.8 collective-permute-start
  108.7 23.0 %collective-permute-done = f32[4,32,1,1024]{3,1,2,0:T(8,128)S(1)} collective-permute-done((f32[4,32,1,1024]{3,1,2,0:T(8,128)S(1)}, f32[4,32,1,1024]{3,1,2,0:T(8,128)S(1)}, u32[]{:S(2)}, u32[]{:S(2)}) %collective-permute-start) | collective-permute-done | bytes 524320 | tf_op jit(solution)/shard_map/ppermute | solution.py:17
  134.7 11.6 %collective-permute-done.1 = f32[4,32,1,1024]{3,1,2,0:T(8,128)S(1)} collective-permute-done((f32[4,32,1,1024]{3,1,2,0:T(8,128)S(1)}, f32[4,32,1,1024]{3,1,2,0:T(8,128)S(1)}, u32[]{:S(2)}, u32[]{:S(2)}) %collective-permute-start.1) | collective-permute-done | bytes 524320 | tf_op jit(solution)/shard_map/ppermute | solution.py:18
  155.8 10.0 %multiply_multiply_fusion.10 = (f32[4,32,4,1024]{3,1,2,0:T(8,128)S(1)}, f32[4,32,4,1024]{3,1,2,0:T(8,128)}) fusion(f32[4,32,5,1024]{3,1,2,0:T(8,128)} %constant_dynamic-update-slice_fusion.2, f32[2,3,32,32]{3,2,1,0:T(8,128)S(1)} %copy-done.26, f32[32,4,4,1024]{3,0,2,1:T(8,128)} %fusion.186, f32[4,4,1024,32]{2,3,1,0:T(8,128)} %fusion.189, ...), kind=kOutput, calls=%fused_computation.86 | convolution fusion | flops 236453888 | bytes 13123584 | tf_op jit(solution)/shard_map/tcxs,cd->tdxs/dot_general | solution.py:94
  165.8 5.8 copy.323
  171.7 9.5 %reshape.153 = f32[16,1,32768]{2,1,0:T(1,128)} reshape(f32[4096,4,32]{2,1,0:T(4,128)} %bitcast.536) | data formatting | bytes 4194304
  181.2 32.7 %all_to_all.101 = f32[16,1,32768]{2,1,0:T(1,128)} all-to-all(f32[16,1,32768]{2,1,0:T(1,128)} %reshape.153), channel_id=1, replica_groups=mesh['tm'=16,'space'=8] {'tm'}, dimensions={0} | all-to-all | bytes 4194304 | tf_op jit(solution)/shard_map/all_to_all | solution.py:135
  213.9 8.6 %reduce.1 = f32[16,32768]{1,0:T(8,128)} reduce(f32[16,1,32768]{2,1,0:T(1,128)} %all_to_all.101, f32[]{:T(128)} %broadcast.353), dimensions={1}, to_apply=%all_to_all.78.reduce_sub_computation | reduce | bytes 4194308 | tf_op jit(solution)/shard_map/all_to_all | solution.py:135
  222.5 7.7 reshape.154
  230.2 8.2 %copy.235 = f32[4,32,16,256]{3,1,0,2:T(8,128)} copy(f32[4,32,16,256]{1,0,3,2:T(4,128)} %bitcast.534) | data formatting | bytes 4194304 | tf_op jit(solution)/shard_map/all_to_all | solution.py:135
  260.4 5.1 collective-permute-start.2
  270.2 23.8 %collective-permute-done.2 = f32[4,32,1,1024]{3,1,2,0:T(8,128)S(1)} collective-permute-done((f32[4,32,1,1024]{3,1,2,0:T(8,128)S(1)}, f32[4,32,1,1024]{3,1,2,0:T(8,128)S(1)}, u32[]{:S(2)}, u32[]{:S(2)}) %collective-permute-start.2) | collective-permute-done | bytes 524320 | tf_op jit(solution)/shard_map/ppermute | solution.py:17
  309.0 9.8 %fusion.26 = f32[4,32,4,1024]{3,1,2,0:T(8,128)S(1)} fusion(f32[4,32,4,1024]{3,2,1,0:T(4,128)} %param.6, f32[4,4,1024,32]{2,3,1,0:T(8,128)} %fusion.20, f32[4,4,1024,32]{2,3,1,0:T(8,128)} %fusion.174, f32[4,32,4,1024]{3,2,1,0:T(4,128)} %reshape.120, f32[4,32,1,1024]{3,1,2,0:T(8,128)} %collective-permute-done.3, ...), kind=kOutput, calls=%fused_computation.38 | convolution fusion | flops 240779264 | bytes 13123584 | tf_op jit(solution)/shard_map/tcxs,cd->tdxs/dot_general | solution.py:94
  320.5 32.4 %all_to_all.102 = f32[16,4,32,256]{3,2,1,0:T(8,128)S(1)} all-to-all(f32[16,4,32,256]{3,2,1,0:T(8,128)S(1)} %fusion.148), channel_id=1, replica_groups=mesh['tm'=16,'space'=8] {'tm'}, dimensions={0} | all-to-all | bytes 4194304 | tf_op jit(solution)/shard_map/all_to_all | solution.py:164
  368.9 4.6 all-to-all-start.5
  377.5 6.9 collective-permute-start.5
  395.3 16.3 %collective-permute-done.4 = f32[4,32,1,1024]{3,1,2,0:T(8,128)S(1)} collective-permute-done((f32[4,32,1,1024]{3,1,2,0:T(8,128)S(1)}, f32[4,32,1,1024]{3,1,2,0:T(8,128)S(1)}, u32[]{:S(2)}, u32[]{:S(2)}) %collective-permute-start.4) | collective-permute-done | bytes 524320 | tf_op jit(solution)/shard_map/ppermute | solution.py:18
  420.1 9.6 %multiply_add_fusion = f32[4,32,4,1024]{3,1,2,0:T(8,128)S(1)} fusion(f32[4,32,4,1024]{3,2,1,0:T(4,128)} %reshape.124, f32[4,4,1024,32]{2,3,1,0:T(8,128)} %fusion.2, f32[4,4,1024,32]{2,3,1,0:T(8,128)} %fusion.172, f32[4,32,4,1024]{3,1,2,0:T(8,128)} %get-tuple-element.30, f32[4,32,4,1024]{3,1,2,0:T(8,128)} %copy-done, ...), kind=kOutput, calls=%fused_computation.57 | convolution fusion | flops 240779264 | bytes 13123584 | tf_op jit(solution)/shard_map/tdxs,cd->tcxs/dot_general | solution.py:108
  440.6 5.1 all-to-all-start.6
  455.6 7.2 collective-permute-start.7
  492.6 5.3 all-to-all-start.7
  498.0 88.0 %psum.15 = f32[2,3,32,32]{3,2,1,0:T(8,128)} all-reduce(f32[2,3,32,32]{3,2,1,0:T(8,128)S(1)} %pad_maximum_fusion.11), channel_id=1, replica_groups=mesh['tm'=16,'space'=8] {'tm','space'}, use_global_device_ids=true, to_apply=%region_2.3 | all-reduce | flops 6144 | bytes 49152 | tf_op jit(solution)/shard_map/psum | solution.py:177
  599.5 112.7 %all-reduce.3.cloned.1.call-done = f32[2,2,16,32,32]{4,3,2,1,0:T(8,128)} async-done(((f32[2,2,16,32,32]{4,3,2,1,0:T(8,128)}), f32[2,2,16,32,32]{4,3,2,1,0:T(8,128)}) %all-reduce.3.cloned.1.call-update) | async-done | bytes 262160
  713.7 43.4 %psum.14 = f32[2,2,1,32,32]{4,3,2,1,0:T(8,128)} all-reduce(f32[2,2,1,32,32]{4,3,2,1,0:T(8,128)S(1)} %constant_dynamic-slice_fusion), channel_id=1, replica_groups=mesh['tm'=16,'space'=8] {'space'}, use_global_device_ids=true, to_apply=%region_1.2 | all-reduce | flops 4096 | bytes 32768 | tf_op jit(solution)/shard_map/psum | solution.py:181
  764.4 6.4 bitcast_add_fusion
  (218 shorter events, 191.9 us)
Async XLA Ops:
  81.2 3.0 copy-start.10
  92.6 4.6 copy-start.2
  92.6 58.0 %all-to-all-start.1 = ((f32[64,32,256]{2,1,0:T(8,128)}), f32[64,32,256]{2,1,0:T(8,128)}, u32[]{:S(2)}, u32[]{:S(2)}) async-start(f32[64,32,256]{2,1,0:T(8,128)} %bitcast.589), calls=%async_computation.1 | async-start | bytes 4194304 | tf_op jit(solution)/shard_map/all_to_all | solution.py:139
  97.2 7.2 copy-start.26
  98.1 33.6 %collective-permute-start = (f32[4,32,1,1024]{3,1,2,0:T(8,128)S(1)}, f32[4,32,1,1024]{3,1,2,0:T(8,128)S(1)}, u32[]{:S(2)}, u32[]{:S(2)}) collective-permute-start(f32[4,32,1,1024]{3,1,2,0:T(8,128)S(1)} %copy.453), channel_id=1, source_target_pairs={{0,1},{1,2},{2,3},{3,4},{4,5},{5,6},{6,7},{8,9},{9,10},{10,11},{11... | collective-permute-start | bytes 1572872 | tf_op jit(solution)/shard_map/ppermute | solution.py:17
  103.1 43.2 %collective-permute-start.1 = (f32[4,32,1,1024]{3,1,2,0:T(8,128)S(1)}, f32[4,32,1,1024]{3,1,2,0:T(8,128)S(1)}, u32[]{:S(2)}, u32[]{:S(2)}) collective-permute-start(f32[4,32,1,1024]{3,1,2,0:T(8,128)S(1)} %copy.454), channel_id=1, source_target_pairs={{1,0},{2,1},{3,2},{4,3},{5,4},{6,5},{7,6},{9,8},{10,9},{11,10},{12... | collective-permute-start | bytes 1572872 | tf_op jit(solution)/shard_map/ppermute | solution.py:18
  134.7 12.4 %copy-start.22 = (f32[4,32,5,1024]{3,1,2,0:T(8,128)}, f32[4,32,5,1024]{3,1,2,0:T(8,128)S(1)}, u32[]{:S(2)}) copy-start(f32[4,32,5,1024]{3,1,2,0:T(8,128)S(1)} %get-tuple-element.24) | copy-start | bytes 7864324
  255.1 43.2 %all-to-all-start.3 = ((f32[64,32,256]{2,1,0:T(8,128)}), f32[64,32,256]{2,1,0:T(8,128)}, u32[]{:S(2)}, u32[]{:S(2)}) async-start(f32[64,32,256]{2,1,0:T(8,128)} %bitcast.590), calls=%async_computation.3 | async-start | bytes 4194304 | tf_op jit(solution)/shard_map/all_to_all | solution.py:139
  260.4 33.6 %collective-permute-start.2 = (f32[4,32,1,1024]{3,1,2,0:T(8,128)S(1)}, f32[4,32,1,1024]{3,1,2,0:T(8,128)S(1)}, u32[]{:S(2)}, u32[]{:S(2)}) collective-permute-start(f32[4,32,1,1024]{3,1,2,0:T(8,128)S(1)} %get-tuple-element.20), channel_id=1, source_target_pairs={{0,1},{1,2},{2,3},{3,4},{4,5},{5,6},{6,7},{8,9},{9,10},{10,11},{11... | collective-permute-start | bytes 1572872 | tf_op jit(solution)/shard_map/ppermute | solution.py:17
  265.6 43.5 %collective-permute-start.3 = (f32[4,32,1,1024]{3,1,2,0:T(8,128)}, f32[4,32,1,1024]{3,1,2,0:T(8,128)}, u32[]{:S(2)}, u32[]{:S(2)}) collective-permute-start(f32[4,32,1,1024]{3,1,2,0:T(8,128)} %get-tuple-element.19), channel_id=1, source_target_pairs={{1,0},{2,1},{3,2},{4,3},{5,4},{6,5},{7,6},{9,8},{10,9},{11,10},{12... | collective-permute-start | bytes 1572872 | tf_op jit(solution)/shard_map/ppermute | solution.py:18
  358.3 3.1 copy-start.16
  368.9 4.6 copy-start.30
  368.9 46.2 %all-to-all-start.5 = ((f32[64,32,256]{2,1,0:T(8,128)}), f32[64,32,256]{2,1,0:T(8,128)}, u32[]{:S(2)}, u32[]{:S(2)}) async-start(f32[64,32,256]{2,1,0:T(8,128)} %bitcast.588), calls=%async_computation.5 | async-start | bytes 4194304 | tf_op jit(solution)/shard_map/all_to_all | solution.py:173
  373.5 10.9 %copy-start.1 = (f32[4,32,4,1024]{3,1,2,0:T(8,128)S(1)}, f32[4,32,4,1024]{3,1,2,0:T(8,128)}, u32[]{:S(2)}) copy-start(f32[4,32,4,1024]{3,1,2,0:T(8,128)} %copy-done) | copy-start | bytes 6291460
  376.2 35.4 %collective-permute-start.4 = (f32[4,32,1,1024]{3,1,2,0:T(8,128)S(1)}, f32[4,32,1,1024]{3,1,2,0:T(8,128)S(1)}, u32[]{:S(2)}, u32[]{:S(2)}) collective-permute-start(f32[4,32,1,1024]{3,1,2,0:T(8,128)S(1)} %get-tuple-element.18), channel_id=1, source_target_pairs={{1,0},{2,1},{3,2},{4,3},{5,4},{6,5},{7,6},{9,8},{10,9},{11,10},{12... | collective-permute-start | bytes 1572872 | tf_op jit(solution)/shard_map/ppermute | solution.py:18
  377.5 42.7 %collective-permute-start.5 = (f32[4,32,1,1024]{3,1,2,0:T(8,128)}, f32[4,32,1,1024]{3,1,2,0:T(8,128)}, u32[]{:S(2)}, u32[]{:S(2)}) collective-permute-start(f32[4,32,1,1024]{3,1,2,0:T(8,128)} %get-tuple-element.17), channel_id=1, source_target_pairs={{0,1},{1,2},{2,3},{3,4},{4,5},{5,6},{6,7},{8,9},{9,10},{10,11},{11... | collective-permute-start | bytes 1572872 | tf_op jit(solution)/shard_map/ppermute | solution.py:17
  440.6 33.0 %all-to-all-start.6 = ((f32[16,4,32,256]{3,2,1,0:T(8,128)}), f32[16,4,32,256]{3,2,1,0:T(8,128)}, u32[]{:S(2)}, u32[]{:S(2)}) async-start(f32[16,4,32,256]{3,2,1,0:T(8,128)} %fusion.132), calls=%async_computation.6 | async-start | bytes 4194304 | tf_op jit(solution)/shard_map/all_to_all | solution.py:164
  445.8 4.6 copy-start.13
  445.8 4.6 copy-start.17
  445.8 5.8 copy-start.9
  445.8 5.8 copy-start.15
  451.7 11.2 %copy-start.3 = (f32[4,32,4,1024]{3,2,1,0:T(4,128)S(1)}, f32[4,32,4,1024]{3,2,1,0:T(4,128)}, u32[]{:S(2)}) copy-start(f32[4,32,4,1024]{3,2,1,0:T(4,128)} %param.5) | copy-start | bytes 6291460
  454.3 140.7 %collective-permute-start.6 = (f32[4,32,1,1024]{3,1,2,0:T(8,128)}, f32[4,32,1,1024]{3,1,2,0:T(8,128)}, u32[]{:S(2)}, u32[]{:S(2)}) collective-permute-start(f32[4,32,1,1024]{3,1,2,0:T(8,128)} %get-tuple-element.16), channel_id=1, source_target_pairs={{1,0},{2,1},{3,2},{4,3},{5,4},{6,5},{7,6},{9,8},{10,9},{11,10},{12... | collective-permute-start | bytes 1572872 | tf_op jit(solution)/shard_map/ppermute | solution.py:18
  455.6 308.8 %collective-permute-start.7 = (f32[4,32,1,1024]{3,1,2,0:T(8,128)}, f32[4,32,1,1024]{3,1,2,0:T(8,128)}, u32[]{:S(2)}, u32[]{:S(2)}) collective-permute-start(f32[4,32,1,1024]{3,1,2,0:T(8,128)} %get-tuple-element.15), channel_id=1, source_target_pairs={{0,1},{1,2},{2,3},{3,4},{4,5},{5,6},{6,7},{8,9},{9,10},{10,11},{11... | collective-permute-start | bytes 1572872 | tf_op jit(solution)/shard_map/ppermute | solution.py:17
  465.8 3.6 copy-start.23
  482.1 3.3 copy-start.20
  492.6 5.4 copy-start.27
  492.6 264.5 %all-to-all-start.7 = ((f32[64,32,256]{2,1,0:T(8,128)}), f32[64,32,256]{2,1,0:T(8,128)}, u32[]{:S(2)}, u32[]{:S(2)}) async-start(f32[64,32,256]{2,1,0:T(8,128)} %bitcast.587), calls=%async_computation.7 | async-start | bytes 4194304 | tf_op jit(solution)/shard_map/all_to_all | solution.py:173
  497.9 214.3 %all-reduce.3.cloned.1.call-start = ((), (), s32[]{:S(2)}) async-start(), calls=%async_computation.8 | async-start | bytes 2097152
  586.0 3.5 copy-start.11
  586.0 3.5 copy-start.19
  586.0 4.7 copy-start.21
  (13 other events, 30.5 us)
Sparse Core Ops, SparseCore 0:
  595.1 117.0 all-reduce.2
